TPU v7x, 256 devices: a whole 4x4x8 slice. The times are simulated.
256 devices in a mesh: px: 8 (over z_hi, core), py: 32 (over z_lo, x, y).
Axes of the slice: x: 4, y: 4, z: 8 (z_hi: 4, z_lo: 2; z = z_hi * 2 + z_lo), core: 2. Of those that a mesh axis runs over, the one named last changes fastest.
Arguments:
- span: float32 [64, 32, 128, 128], P(None, 'px', 'py'), may hold values from -4 to 4
- potential: float32 [32, 128, 128], P('px', 'py'), may hold values from 0.1 to 2
- cell_matrix: float32 [125, 125], replicated, may hold values from -2 to 7, as said below
- block: bfloat16 [256, 32, 128, 128], P(None, 'px', 'py'), may hold values from -0.015625 to 0.015625
Outputs:
- filtered: float32 [64, 32, 128, 128], P(None, 'px', 'py')
- margin: float32 [64, 256], P('px', 'py')
Inputs may be any that keep to these rules, and one draw needn't show every extreme that they name: `cell_matrix`: symmetric.
All inputs are finite; a program needn't handle non-finite values.
Results may differ from a plain program's by a relative error of at most 0.0029.
Values sent between devices are 32-bit elements; how exact they have to be, the bound alone decides.
A program may use at most 128 MiB of HBM per device.

v0:
```python
import functools

import jax
import jax.numpy as jnp
from jax import lax
from jax.experimental import pallas as pl
from jax.experimental.pallas import tpu as pltpu
from jax.sharding import PartitionSpec as P

MESH = pl.DeviceIdType.MESH
CENTRE = 13.0
SCALE = 2.0 / 9.0
F32 = jnp.float32
BF16 = jnp.bfloat16
CHUNKS = 2


def rows_to_lanes(parts, width):
    count = len(parts)
    parts = list(parts)
    group = lax.broadcasted_iota(jnp.int32, parts[0].shape, 1) // width
    bit = count // 2
    while bit:
        low = (group & bit) == 0
        for first in range(count):
            if first & bit:
                continue
            a, b = parts[first], parts[first | bit]
            parts[first] = jnp.where(low, a, pltpu.roll(b, bit * width, 1))
            parts[first | bit] = jnp.where(low, pltpu.roll(a, 128 - bit * width, 1), b)
        bit //= 2
    return parts


def kernel(
    px_size, py_size, chunks,
    span_hbm, pot_ref, mat_ref, block_hbm,
    out_hbm, tile_ref,
    span_v, block_v, block_f, block_k, mat_pad, mat3, diag,
    v0, v1, v2, c1, c2, c3, r1, r2, r3,
    out_v, lhs, part, got1, sum1, got2,
    in_sem, out_sem, send_sem, recv_sem, send1, recv1, send2, recv2,
):
    states = 64
    width = states // chunks
    groups = 128 // width
    rows = 128 // groups
    px, py = lax.axis_index("px"), lax.axis_index("py")
    xn, xp = lax.rem(px + 1, px_size), lax.rem(px + px_size - 1, px_size)
    yn, yp = lax.rem(py + 1, py_size), lax.rem(py + py_size - 1, py_size)
    tile_rows = states // px_size
    tile_cols = 256 // py_size
    per_block = 128 // tile_cols

    load_span = pltpu.make_async_copy(span_hbm, span_v, in_sem.at[0])
    load_block = pltpu.make_async_copy(block_hbm, block_v, in_sem.at[1])
    load_span.start()
    load_block.start()

    barrier = pltpu.get_barrier_semaphore()

    def greet(x, y):
        pl.semaphore_signal(barrier, inc=1, device_id=(x, y), device_id_type=MESH)

    for x, y in ((xn, yn), (xn, yp), (xp, yn), (xp, yp)):
        greet(x, y)
    for step in range(1, px_size):
        greet(lax.rem(px + step, px_size), py)

    def greet_y(step, carry):
        greet(px, lax.rem(py + step, py_size))
        return carry

    lax.fori_loop(1, py_size, greet_y, 0)

    def flat(ref, c):
        return ref.at[c].reshape(35 * rows, 128)

    load_span.wait()
    for c in range(chunks):
        for ref in (v0, v1, v2):
            ref[c, 5:7] = jnp.zeros((2, 5, rows, 128), F32)
        for x in range(4):
            for y0 in range(0, 4, groups):
                count = min(groups, 4)
                stack = jnp.concatenate(
                    [span_v[pl.ds(c * width * 16 + x * 4 + y0 + i, width, stride=16), :] for i in range(count)], 0
                )
                turned = stack.T
                pieces = rows_to_lanes([turned[h * rows:(h + 1) * rows] for h in range(groups)], width)
                for i in range(count):
                    v0[c, x, y0 + i] = pieces[i]

    pl.semaphore_wait(barrier, 4 + (px_size - 1) + (py_size - 1))

    def remote(src, dst, c, slot, x, y):
        copy = pltpu.make_async_remote_copy(
            src_ref=src, dst_ref=dst, send_sem=send_sem.at[c, slot], recv_sem=recv_sem.at[c, slot],
            device_id=(x, y), device_id_type=MESH,
        )
        copy.start()
        return copy

    halo, exchange1, exchange2, last = [], [], [], []
    for c in range(chunks):
        halo.append([
            remote(v0.at[c, 0, 0:4], v0.at[c, 4, 0:4], c, 0, xp, py),
            remote(v0.at[c, 0:4, 0], v0.at[c, 0:4, 4], c, 1, px, yp),
            remote(v0.at[c, 0, 0], v0.at[c, 4, 4], c, 2, xp, yp),
        ])

    def exchange(contrib, got, c, base):
        return [
            remote(contrib.at[c, 4, 0:5], got.at[c, 0:5], c, base, xn, py),
            remote(contrib.at[c, 0, 0:5], got.at[c, 5:10], c, base + 1, xp, py),
            remote(contrib.at[c, 0:5, 4], got.at[c, 10:15], c, base + 2, px, yn),
            remote(contrib.at[c, 0:5, 0], got.at[c, 15:20], c, base + 3, px, yp),
            remote(contrib.at[c, 4, 4], got.at[c, 20], c, base + 4, xn, yn),
            remote(contrib.at[c, 4, 0], got.at[c, 21], c, base + 5, xn, yp),
            remote(contrib.at[c, 0, 4], got.at[c, 22], c, base + 6, xp, yn),
            remote(contrib.at[c, 0, 0], got.at[c, 23], c, base + 7, xp, yp),
        ]

    def send_last(c, base):
        return [
            remote(c3.at[c, 4, 0:4], r3.at[c, 0:4], c, base, xn, py),
            remote(c3.at[c, 0:4, 4], r3.at[c, 4:8], c, base + 1, px, yn),
            remote(c3.at[c, 4, 4], r3.at[c, 8], c, base + 2, xn, yn),
        ]

    mat_pad[...] = jnp.zeros((128, 128), F32)
    mat_pad[0:125, 0:125] = mat_ref[...]
    scaled = mat_pad[...] * SCALE
    mat_hi = scaled.astype(BF16)
    mat_lo = (scaled - mat_hi.astype(F32)).astype(BF16)
    i = lax.broadcasted_iota(jnp.int32, (160, 128), 0)
    a = lax.broadcasted_iota(jnp.int32, (160, 128), 1)
    pick = jnp.where((i % 32 < 25) & (a == (i % 32) * 5 + i // 32), 1.0, 0.0).astype(BF16)
    j = lax.broadcasted_iota(jnp.int32, (128, 480), 1)
    b = lax.broadcasted_iota(jnp.int32, (128, 480), 0)
    jj = j % 160
    hit = (jj % 32 < 25) & (b == (jj % 32) * 5 + jj // 32)
    middle = (j >= 160) & (j < 320)
    put_hi = jnp.where(hit & jnp.logical_not(middle), 1.0, 0.0).astype(BF16)
    put_lo = jnp.where(hit & middle, 1.0, 0.0).astype(BF16)
    row_hi = jnp.dot(pick, mat_hi, preferred_element_type=F32).astype(BF16)
    row_lo = jnp.dot(pick, mat_lo, preferred_element_type=F32).astype(BF16)
    mat3[...] = (
        jnp.dot(row_hi, put_hi, preferred_element_type=F32) + jnp.dot(row_lo, put_lo, preferred_element_type=F32)
    ).astype(BF16)

    diag[...] = jnp.zeros((7, 5, rows, 128), F32)
    pot = (jnp.concatenate([pot_ref[...], jnp.zeros((112, 128), F32)], 0) - CENTRE) * SCALE
    pot = pot.T
    lane_group = lax.broadcasted_iota(jnp.int32, (rows, 128), 1) // width
    for x in range(4):
        for y in range(4):
            column = jnp.broadcast_to(pot[:, x * 4 + y:x * 4 + y + 1], (128, 128))
            value = column[0:rows]
            for h in range(1, groups):
                value = jnp.where(lane_group == h, column[h * rows:(h + 1) * rows], value)
            diag[x, y] = value

    load_block.wait()

    def widen(step, carry):
        at = pl.ds(pl.multiple_of(step * 256, 256), 256)
        block_f[at, :] = block_v[at, :].astype(F32)
        return carry

    lax.fori_loop(0, 16, widen, 0)
    for node in range(16):
        block_k[:, node * 128:(node + 1) * 128] = block_f[pl.ds(node, 256, stride=16), :].astype(BF16)

    def apply(source, contrib, c):
        src, dst, dia = flat(source, c), flat(contrib, c), diag.reshape(35 * rows, 128)
        high, low, full = [], [], []
        for r in range(rows):
            full.append(src[pl.ds(r, 32, stride=rows), :])
        full.append(pltpu.roll(full[0], 128 - width, 1))
        for value in full:
            h = value.astype(BF16)
            high.append(h)
            low.append((value - h.astype(F32)).astype(BF16))
        carry = None
        first_row = None
        for k in range(0, rows // 4, 2):
            rhs = jnp.concatenate([
                jnp.concatenate(
                    high[4 * n:4 * n + 5] + high[4 * n:4 * n + 5] + low[4 * n:4 * n + 5], 0
                ) for n in (k, k + 1)
            ], 1)
            product = jnp.dot(mat3[...], rhs, preferred_element_type=F32)
            for n in (0, 1):
                mine = product[:, n * 128:(n + 1) * 128]
                for z in range(4):
                    r = 4 * (k + n) + z
                    value = mine[z * 32:(z + 1) * 32] + dia[pl.ds(r, 32, stride=rows), :] * full[r]
                    if z == 0 and carry is not None:
                        value = value + carry
                    if r == 0:
                        first_row = value
                    else:
                        dst[pl.ds(r, 32, stride=rows), :] = value
                carry = mine[128:160]
        dst[pl.ds(0, 32, stride=rows), :] = first_row + pltpu.roll(carry, width, 1)

    def assemble(contrib, got, c, x, y):
        value = contrib[c, x, y]
        if x == 0:
            value = value + got[c, y]
        if x == 4:
            value = value + got[c, 5 + y]
        if y == 0:
            value = value + got[c, 10 + x]
        if y == 4:
            value = value + got[c, 15 + x]
        corner = {(0, 0): 20, (0, 4): 21, (4, 0): 22, (4, 4): 23}.get((x, y))
        if corner is not None:
            value = value + got[c, corner]
        return value

    for c in range(chunks):
        for copy in halo[c]:
            copy.wait_recv()
        apply(v0, c1, c)
        exchange1.append(exchange(c1, r1, c, 3))
    for c in range(chunks):
        for copy in exchange1[c]:
            copy.wait_recv()
        for x in range(5):
            for y in range(5):
                v1[c, x, y] = 0.5 * assemble(c1, r1, c, x, y)
        apply(v1, c2, c)
        exchange2.append(exchange(c2, r2, c, 11))
    for c in range(chunks):
        for copy in exchange2[c]:
            copy.wait_recv()
        for x in range(5):
            for y in range(5):
                v2[c, x, y] = assemble(c2, r2, c, x, y) - v0[c, x, y]
        apply(v2, c3, c)
        last.append(send_last(c, 19))

    def first_copy(owner):
        return pltpu.make_async_remote_copy(
            src_ref=part.at[owner], dst_ref=got1.at[px], send_sem=send1.at[owner], recv_sem=recv1.at[px],
            device_id=(owner, py), device_id_type=MESH,
        )

    stores = []
    per_chunk = width // tile_rows
    for c in range(chunks):
        for copy in last[c]:
            copy.wait_recv()
        for x in range(4):
            values = []
            for y in range(4):
                value = c3[c, x, y] - v1[c, x, y]
                if x == 0:
                    value = value + r3[c, y]
                if y == 0:
                    value = value + r3[c, 4 + x]
                if x == 0 and y == 0:
                    value = value + r3[c, 8]
                values.append(value)
            for y0 in range(0, 4, groups):
                pieces = rows_to_lanes(values[y0:y0 + groups], width)
                turned = jnp.concatenate(pieces, 0).T
                for i in range(groups):
                    node = x * 4 + y0 + i
                    value = turned[i * width:(i + 1) * width]
                    out_v[pl.ds(c * width * 16 + node, width, stride=16), :] = value
                    lhs[c, :, node * 128:(node + 1) * 128] = value.astype(BF16)
        at = pl.ds(c * width * 16, width * 16)
        store = pltpu.make_async_copy(out_v.at[at], out_hbm.at[at], out_sem.at[c])
        store.start()
        stores.append(store)
        product = lax.dot_general(lhs[c], block_k[...], (((1,), (1,)), ((), ())), preferred_element_type=F32)
        for n in range(per_chunk):
            owner = c * per_chunk + n
            part[owner] = product[n * tile_rows:(n + 1) * tile_rows]

            @pl.when(px != owner)
            def _():
                first_copy(owner).start()

            @pl.when(px == owner)
            def _():
                got1[px] = part[owner]

    for step in range(1, px_size):
        source = lax.rem(px + step, px_size)
        pltpu.make_async_remote_copy(
            src_ref=part.at[0], dst_ref=got1.at[source], send_sem=send1.at[source], recv_sem=recv1.at[source],
            device_id=(source, py), device_id_type=MESH,
        ).wait_recv()
    total = got1[0]
    for n in range(1, px_size):
        total = total + got1[n]
    sum1[0] = total[:, 0:128]
    sum1[1] = total[:, 128:256]

    def second_copy(target):
        return pltpu.make_async_remote_copy(
            src_ref=sum1.at[target // per_block], dst_ref=got2.at[py], send_sem=send2.at[target], recv_sem=recv2.at[py],
            device_id=(px, target), device_id_type=MESH,
        )

    def send_second(step, carry):
        second_copy(lax.rem(py + step, py_size)).start()
        return carry

    lax.fori_loop(1, py_size, send_second, 0)
    got2[py] = sum1[py // per_block]

    def wait_second(step, carry):
        source = lax.rem(py + step, py_size)
        pltpu.make_async_remote_copy(
            src_ref=sum1.at[0], dst_ref=got2.at[source], send_sem=send2.at[source], recv_sem=recv2.at[source],
            device_id=(px, source), device_id_type=MESH,
        ).wait_recv()
        return carry

    lax.fori_loop(1, py_size, wait_second, 0)
    total = got2[0]
    for n in range(1, py_size):
        total = total + got2[n]
    shift = lax.rem(128 - lax.rem(py, per_block) * tile_cols, 128)
    tile_ref[...] = pltpu.roll(total, shift, 1)[:, 0:tile_cols]

    for store in stores:
        store.wait()
    for c in range(chunks):
        for copy in halo[c] + exchange1[c] + exchange2[c] + last[c]:
            copy.wait_send()
    for step in range(1, px_size):
        owner = lax.rem(px + step, px_size)
        first_copy(owner).wait_send()

    def wait_sent(step, carry):
        second_copy(lax.rem(py + step, py_size)).wait_send()
        return carry

    lax.fori_loop(1, py_size, wait_sent, 0)


def local(px_size, py_size, span, potential, cell_matrix, block):
    chunks = CHUNKS
    width = 64 // chunks
    rows = width
    field = pltpu.VMEM((chunks, 7, 5, rows, 128), F32)
    tile = (64 // px_size, 256 // py_size)
    filtered, margin = pl.pallas_call(
        functools.partial(kernel, px_size, py_size, chunks),
        out_shape=(jax.ShapeDtypeStruct((1024, 128), F32), jax.ShapeDtypeStruct(tile, F32)),
        in_specs=[
            pl.BlockSpec(memory_space=pl.ANY),
            pl.BlockSpec(memory_space=pltpu.VMEM),
            pl.BlockSpec(memory_space=pltpu.VMEM),
            pl.BlockSpec(memory_space=pl.ANY),
        ],
        out_specs=(pl.BlockSpec(memory_space=pl.ANY), pl.BlockSpec(memory_space=pltpu.VMEM)),
        scratch_shapes=[
            pltpu.VMEM((1024, 128), F32),
            pltpu.VMEM((4096, 128), BF16),
            pltpu.VMEM((4096, 128), F32),
            pltpu.VMEM((256, 2048), BF16),
            pltpu.VMEM((128, 128), F32),
            pltpu.VMEM((160, 480), BF16),
            pltpu.VMEM((7, 5, rows, 128), F32),
            field, field, field, field, field, field,
            pltpu.VMEM((chunks, 24, rows, 128), F32),
            pltpu.VMEM((chunks, 24, rows, 128), F32),
            pltpu.VMEM((chunks, 9, rows, 128), F32),
            pltpu.VMEM((1024, 128), F32),
            pltpu.VMEM((chunks, width, 2048), BF16),
            pltpu.VMEM((px_size, tile[0], 256), F32),
            pltpu.VMEM((px_size, tile[0], 256), F32),
            pltpu.VMEM((2, tile[0], 128), F32),
            pltpu.VMEM((py_size, tile[0], 128), F32),
            pltpu.SemaphoreType.DMA((2,)),
            pltpu.SemaphoreType.DMA((chunks,)),
            pltpu.SemaphoreType.DMA((chunks, 22)),
            pltpu.SemaphoreType.DMA((chunks, 22)),
            pltpu.SemaphoreType.DMA((px_size,)),
            pltpu.SemaphoreType.DMA((px_size,)),
            pltpu.SemaphoreType.DMA((py_size,)),
            pltpu.SemaphoreType.DMA((py_size,)),
        ],
        compiler_params=pltpu.CompilerParams(
            collective_id=0, has_side_effects=True, vmem_limit_bytes=48 * 1024 * 1024
        ),
    )(span.reshape(1024, 128), potential.reshape(16, 128), cell_matrix, block.reshape(4096, 128))
    return filtered.reshape(span.shape), margin


def solution(mesh):
    in_specs = (P(None, "px", "py", None), P("px", "py", None), P(), P(None, "px", "py", None))
    out_specs = (P(None, "px", "py", None), P("px", "py"))
    body = functools.partial(local, mesh.shape["px"], mesh.shape["py"])
    return jax.shard_map(body, mesh=mesh, in_specs=in_specs, out_specs=out_specs, check_vma=False)
```

profile of v0, /device:TPU:1, one launch (start us, length us, event | category | flops | bytes accessed | tf_op | source)
XLA Modules:
  0.0 68.5 jit_solution(16663818199932232107)
XLA Ops:
  0.6 0.0 copy-start
  0.6 1.2 %copy-done = bf16[256,4,4,128]{3,2,1,0:T(4,128)(2,1)S(1)} copy-done((bf16[256,4,4,128]{3,2,1,0:T(4,128)(2,1)S(1)}, bf16[256,4,4,128]{3,2,1,0:T(4,128)(2,1)}, u32[]{:S(2)}) %copy-start) | copy-done | bytes 1048600
  1.9 0.0 copy-start.1
  1.9 1.0 %copy-done.1 = f32[64,4,4,128]{3,2,1,0:T(4,128)S(1)} copy-done((f32[64,4,4,128]{3,2,1,0:T(4,128)S(1)}, f32[64,4,4,128]{3,2,1,0:T(4,128)}, u32[]{:S(2)}) %copy-start.1) | copy-done | bytes 524312
  2.9 0.0 copy-start.2
  2.9 0.8 %copy-done.2 = f32[125,125]{1,0:T(8,128)S(1)} copy-done((f32[125,125]{1,0:T(8,128)S(1)}, f32[125,125]{1,0:T(8,128)}, u32[]{:S(2)}) %copy-start.2) | copy-done | bytes 62524
  3.7 0.0 copy-start.3
  3.7 0.7 %copy-done.3 = f32[4,4,128]{2,1,0:T(4,128)S(1)} copy-done((f32[4,4,128]{2,1,0:T(4,128)S(1)}, f32[4,4,128]{2,1,0:T(4,128)}, u32[]{:S(2)}) %copy-start.3) | copy-done | bytes 8216
  4.4 62.6 %shard_map.59 = (f32[1024,128]{1,0:T(8,128)S(1)}, f32[8,8]{1,0:T(8,128)S(1)}) custom-call(f32[1024,128]{1,0:T(8,128)S(1)} %bitcast.5, f32[16,128]{1,0:T(8,128)S(1)} %bitcast.7, f32[125,125]{1,0:T(8,128)S(1)} %copy-done.2, bf16[4096,128]{1,0:T(8,128)(2,1)S(1)} %bitcast.4), custom_call_target="tpu_custom_call" | custom-call | tf_op jit(solution)/shard_map/pallas_call | solution.py:354
  67.1 0.8 %copy.8 = f32[64,4,4,128]{3,2,1,0:T(4,128)} copy(f32[64,4,4,128]{3,2,1,0:T(4,128)S(1)} %bitcast.6) | data formatting | bytes 1048576
  67.9 0.6 copy.9
Async XLA Ops:
  0.6 1.2 %copy-start = (bf16[256,4,4,128]{3,2,1,0:T(4,128)(2,1)S(1)}, bf16[256,4,4,128]{3,2,1,0:T(4,128)(2,1)}, u32[]{:S(2)}) copy-start(bf16[256,4,4,128]{3,2,1,0:T(4,128)(2,1)} %param.7) | copy-start | bytes 3145732
  1.9 1.0 %copy-start.1 = (f32[64,4,4,128]{3,2,1,0:T(4,128)S(1)}, f32[64,4,4,128]{3,2,1,0:T(4,128)}, u32[]{:S(2)}) copy-start(f32[64,4,4,128]{3,2,1,0:T(4,128)} %param.4) | copy-start | bytes 1572868
  2.9 0.8 %copy-start.2 = (f32[125,125]{1,0:T(8,128)S(1)}, f32[125,125]{1,0:T(8,128)}, u32[]{:S(2)}) copy-start(f32[125,125]{1,0:T(8,128)} %mat_ref.1) | copy-start | bytes 187504
  3.7 0.7 %copy-start.3 = (f32[4,4,128]{2,1,0:T(4,128)S(1)}, f32[4,4,128]{2,1,0:T(4,128)}, u32[]{:S(2)}) copy-start(f32[4,4,128]{2,1,0:T(4,128)} %param.5) | copy-start | bytes 24580
where the time goes:
time: 69.4 us; the launch traced here: 68.5 us
  Pallas kernels  62.6 us (90%)
  local copies, waits for them, and re-layouts  5.18 us (7%)
    pallas_call x1, Pallas kernels, local(): pl.pallas_call(functools.partial(kernel, px_size, py_size, chunks), out_s...  62.6 us
    unnamed x10, local copies, waits for them, and re-layouts  5.18 us

commit v1 on v0

v1 whole, which is shorter than its diff:
```python
import functools

import jax
import jax.numpy as jnp
from jax import lax
from jax.experimental import pallas as pl
from jax.experimental.pallas import tpu as pltpu
from jax.sharding import PartitionSpec as P

MESH = pl.DeviceIdType.MESH
CENTRE = 13.0
SCALE = 2.0 / 9.0
F32 = jnp.float32
BF16 = jnp.bfloat16
CHUNKS = 1
STATES = 64
BLOCK = 256


def rows_to_lanes(parts, width):
    count = len(parts)
    parts = list(parts)
    group = lax.broadcasted_iota(jnp.int32, parts[0].shape, 1) // width
    bit = count // 2
    while bit:
        low = (group & bit) == 0
        for first in range(count):
            if first & bit:
                continue
            a, b = parts[first], parts[first | bit]
            parts[first] = jnp.where(low, a, pltpu.roll(b, bit * width, 1))
            parts[first | bit] = jnp.where(low, pltpu.roll(a, 128 - bit * width, 1), b)
        bit //= 2
    return parts


def kernel(
    px_size, py_size, chunks,
    span_hbm, pot_hbm, mat_hbm, block_hbm,
    out_hbm, tile_ref,
    span_v, mat_v, mat_pad, block_v, block_f, block_k, mat3, diag,
    spans, pots, halo, face_out,
    v0, v1, v2, c1, c2, c3, r1, r2,
    send_back, send_edge, edge, result, lhs, part, got1, sum1, got2,
    ready, local_sem, send_sem, recv_sem, face_send, face_recv, send1, recv1, send2, recv2,
):
    own = STATES // py_size
    per = own // chunks
    width = per * py_size
    groups = 128 // width
    rows = 128 // groups
    px, py = lax.axis_index("px"), lax.axis_index("py")
    xn, xp = lax.rem(px + 1, px_size), lax.rem(px + px_size - 1, px_size)
    tile_rows = STATES // px_size
    tile_cols = BLOCK // py_size
    per_block = 128 // tile_cols

    load_span = pltpu.make_async_copy(span_hbm, span_v, local_sem.at[0])
    load_block = pltpu.make_async_copy(block_hbm, block_v, local_sem.at[1])
    load_mat = pltpu.make_async_copy(mat_hbm, mat_v, local_sem.at[2])
    load_pot = pltpu.make_async_copy(pot_hbm, pots.at[py], local_sem.at[3])
    load_span.start()

    barrier = pltpu.get_barrier_semaphore()

    def greet_y(step, carry):
        pl.semaphore_signal(
            barrier, inc=1, device_id=(px, lax.rem(py + step, py_size)), device_id_type=MESH
        )
        return carry

    def greet_x(step, carry):
        pl.semaphore_signal(
            barrier, inc=1, device_id=(lax.rem(px + step, px_size), py), device_id_type=MESH
        )
        return carry

    lax.fori_loop(1, px_size, greet_x, 0)
    lax.fori_loop(1, py_size, greet_y, 0)
    mat_pad[...] = jnp.zeros((128, 128), F32)
    load_mat.start()
    load_pot.start()
    load_block.start()

    load_span.wait()
    for s in range(own):
        for y in range(4):
            face_out[pl.ds(s * 4 + y, py_size, stride=8), :] = span_v[pl.ds(s * 16 + y, py_size, stride=own * 16), :]

    pl.semaphore_wait(barrier, (px_size - 1) + (py_size - 1))
    for x in (xn, xp):
        pl.semaphore_signal(ready, inc=1, device_id=(x, py), device_id_type=MESH)

    def block_of(ref, index, size):
        return ref.at[pl.ds(pl.multiple_of(index * size, size), size)]

    def send(src, dst, slot, x, y):
        return pltpu.make_async_remote_copy(
            src_ref=src, dst_ref=dst, send_sem=send_sem.at[slot], recv_sem=recv_sem.at[slot],
            device_id=(x, y), device_id_type=MESH,
        )

    def span_copy(target):
        return send(block_of(span_v, target, own * 16), block_of(spans, py, own * 16), 0, px, target)

    def halo_copy(target):
        return send(block_of(face_out, target, 8), block_of(halo, py, 8), 1, xp, target)

    def pot_copy(target):
        return send(pot_hbm, pots.at[py], 2, px, target)

    def over_others(make):
        def body(step, carry):
            make(lax.rem(py + step, py_size)).start()
            return carry

        lax.fori_loop(1, py_size, body, 0)

    def over_all(make):
        def body(step, carry):
            make(lax.rem(py + step, py_size)).start()
            return carry

        lax.fori_loop(0, py_size, body, 0)

    over_others(span_copy)
    pl.semaphore_wait(ready, 2)
    over_all(halo_copy)
    over_others(pot_copy)
    block_of(spans, py, own * 16)[...] = block_of(span_v, py, own * 16)[...]

    load_mat.wait()
    mat_pad[0:125, 0:125] = mat_v[...]
    scaled = mat_pad[...] * SCALE
    mat_hi = scaled.astype(BF16)
    mat_lo = (scaled - mat_hi.astype(F32)).astype(BF16)
    i = lax.broadcasted_iota(jnp.int32, (160, 128), 0)
    a = lax.broadcasted_iota(jnp.int32, (160, 128), 1)
    pick = jnp.where((i % 32 < 25) & (a == (i % 32) * 5 + i // 32), 1.0, 0.0).astype(BF16)
    j = lax.broadcasted_iota(jnp.int32, (128, 480), 1)
    b = lax.broadcasted_iota(jnp.int32, (128, 480), 0)
    jj = j % 160
    hit = (jj % 32 < 25) & (b == (jj % 32) * 5 + jj // 32)
    middle = (j >= 160) & (j < 320)
    put_hi = jnp.where(hit & jnp.logical_not(middle), 1.0, 0.0).astype(BF16)
    put_lo = jnp.where(hit & middle, 1.0, 0.0).astype(BF16)
    row_hi = jnp.dot(pick, mat_hi, preferred_element_type=F32).astype(BF16)
    row_lo = jnp.dot(pick, mat_lo, preferred_element_type=F32).astype(BF16)
    mat3[...] = (
        jnp.dot(row_hi, put_hi, preferred_element_type=F32) + jnp.dot(row_lo, put_lo, preferred_element_type=F32)
    ).astype(BF16)

    for c in range(chunks):
        for ref in (v0, v1, v2):
            ref[c, 5:7] = jnp.zeros((2, 5, rows, 128), F32)

    load_block.wait()

    def widen(step, carry):
        at = pl.ds(pl.multiple_of(step * 256, 256), 256)
        block_f[at, :] = block_v[at, :].astype(F32)
        return carry

    lax.fori_loop(0, BLOCK * 16 // 256, widen, 0)
    for node in range(16):
        block_k[:, node * 128:(node + 1) * 128] = block_f[pl.ds(node, BLOCK, stride=16), :].astype(BF16)

    lane = lax.broadcasted_iota(jnp.int32, (rows, 128), 1)
    first_cell = lax.rem(lane, py_size) == 0
    last_cell = lax.rem(lane, py_size) == py_size - 1

    def from_next(value):
        return jnp.where(last_cell, pltpu.roll(value, py_size - 1, 1), pltpu.roll(value, 127, 1))

    def from_previous(value):
        return jnp.where(first_cell, pltpu.roll(value, 129 - py_size, 1), pltpu.roll(value, 1, 1))

    def turn_in(loads):
        turned = jnp.concatenate(loads, 0).T
        return rows_to_lanes([turned[h * rows:(h + 1) * rows] for h in range(groups)], width)

    def turn_out(values):
        turned = jnp.concatenate(rows_to_lanes(values, width), 0).T
        return [turned[i * width:(i + 1) * width] for i in range(groups)]

    def states_of(ref, c, pitch, per_state, node):
        loads = [
            ref[pl.ds((c * per + s) * per_state + node, py_size, stride=pitch), :] for s in range(per)
        ]
        return jnp.concatenate(loads, 0) if per > 1 else loads[0]

    def flat(ref, c):
        return ref.at[c].reshape(35 * rows, 128)

    def apply(source, contrib, c):
        src, dst = flat(source, c), flat(contrib, c)
        high, low = [], []
        first = None
        for r in range(rows + 1):
            if r < rows:
                value = src[pl.ds(r, 32, stride=rows), :]
                if r == 0:
                    first = value
            else:
                value = pltpu.roll(first, 128 - width, 1)
            h = value.astype(BF16)
            high.append(h)
            low.append((value - h.astype(F32)).astype(BF16))
        carry = None
        first_row = None
        for k in range(0, rows // 4, 2):
            rhs = jnp.concatenate([
                jnp.concatenate(
                    high[4 * n:4 * n + 5] + high[4 * n:4 * n + 5] + low[4 * n:4 * n + 5], 0
                ) for n in (k, k + 1)
            ], 1)
            product = jnp.dot(mat3[...], rhs, preferred_element_type=F32)
            for n in (0, 1):
                mine = product[:, n * 128:(n + 1) * 128]
                for z in range(4):
                    r = 4 * (k + n) + z
                    value = mine[z * 32:(z + 1) * 32]
                    if z == 0 and carry is not None:
                        value = value + carry
                    if r == 0:
                        first_row = value
                    else:
                        dst[pl.ds(r, 32, stride=rows), :] = value
                carry = mine[128:160]
        dst[pl.ds(0, 32, stride=rows), :] = first_row + pltpu.roll(carry, width, 1)

    def folded(contrib, source, c, x, y):
        value = contrib[c, x, y]
        if y == 0:
            value = value + from_previous(contrib[c, x, 4])
        if x < 4:
            value = value + diag[x, y] * source[c, x, y]
        return value

    def face(src, dst, c, slot, x):
        return pltpu.make_async_remote_copy(
            src_ref=src, dst_ref=dst, send_sem=face_send.at[c, slot], recv_sem=face_recv.at[c, slot],
            device_id=(x, py), device_id_type=MESH,
        )

    def send_faces(contrib, source, got, c, base):
        for x in (0, 4):
            for y in range(4):
                contrib[c, x, y] = folded(contrib, source, c, x, y)
        copies = [
            face(contrib.at[c, 4, 0:4], got.at[c, 0], c, base, xn),
            face(contrib.at[c, 0, 0:4], got.at[c, 1], c, base + 1, xp),
        ]
        for copy in copies:
            copy.start()
        return copies

    def place(target, c, x, y, value):
        target[c, x, y] = value
        if y == 0:
            target[c, x, 4] = from_next(value)

    faces = []

    block_wait = pltpu.make_async_remote_copy(
        src_ref=spans.at[pl.ds(0, (py_size - 1) * own * 16)], dst_ref=spans.at[pl.ds(0, (py_size - 1) * own * 16)],
        send_sem=send_sem.at[0], recv_sem=recv_sem.at[0], device_id=(xn, py), device_id_type=MESH,
    )
    halo_wait = pltpu.make_async_remote_copy(
        src_ref=halo, dst_ref=halo, send_sem=send_sem.at[1], recv_sem=recv_sem.at[1],
        device_id=(xn, py), device_id_type=MESH,
    )
    pot_wait = pltpu.make_async_remote_copy(
        src_ref=pots.at[0:py_size - 1], dst_ref=pots.at[0:py_size - 1], send_sem=send_sem.at[2],
        recv_sem=recv_sem.at[2], device_id=(xn, py), device_id_type=MESH,
    )
    block_wait.wait_recv()
    for c in range(chunks):
        for x in range(4):
            for y0 in range(0, 4, groups):
                pieces = turn_in([states_of(spans, c, own * 16, 16, x * 4 + y0 + i) for i in range(groups)])
                for i in range(groups):
                    place(v0, c, x, y0 + i, pieces[i])
    halo_wait.wait_recv()
    for c in range(chunks):
        for y0 in range(0, 4, groups):
            pieces = turn_in([states_of(halo, c, 8, 4, y0 + i) for i in range(groups)])
            for i in range(groups):
                place(v0, c, 4, y0 + i, pieces[i])
        apply(v0, c1, c)
        if c == 0:
            load_pot.wait()
            pot_wait.wait_recv()
            flat_pots = pots.reshape(py_size * 16, 128)
            for x in range(4):
                for y0 in range(0, 4, groups):
                    loads = []
                    for i in range(groups):
                        value = (flat_pots[pl.ds(x * 4 + y0 + i, py_size, stride=16), :] - CENTRE) * SCALE
                        loads += [value] * per
                    pieces = turn_in(loads)
                    for i in range(groups):
                        diag[x, y0 + i] = pieces[i]
        faces.append(send_faces(c1, v0, r1, c, 0))
    for c in range(chunks):
        for x in (1, 2, 3):
            for y in range(4):
                place(v1, c, x, y, 0.5 * folded(c1, v0, c, x, y))

    waiting = faces
    faces = []
    for c in range(chunks):
        for copy in waiting[c]:
            copy.wait_recv()
        for x, n in ((0, 0), (4, 1)):
            for y in range(4):
                place(v1, c, x, y, 0.5 * (c1[c, x, y] + r1[c, n, y]))
        apply(v1, c2, c)
        faces.append(send_faces(c2, v1, r2, c, 2))
    for c in range(chunks):
        for x in (1, 2, 3):
            for y in range(4):
                place(v2, c, x, y, folded(c2, v1, c, x, y) - v0[c, x, y])
    sent = waiting + faces

    waiting = faces
    for c in range(chunks):
        for copy in waiting[c]:
            copy.wait_recv()
        for x, n in ((0, 0), (4, 1)):
            for y in range(4):
                place(v2, c, x, y, c2[c, x, y] + r2[c, n, y] - v0[c, x, y])
        apply(v2, c3, c)
        for x in range(5):
            for y0 in range(0, 4, groups):
                values = []
                for i in range(groups):
                    value = folded(c3, v2, c, x, y0 + i)
                    if x < 4:
                        value = value - v1[c, x, y0 + i]
                    values.append(value)
                pieces = turn_out(values)
                for i in range(groups):
                    for s in range(per):
                        piece = pieces[i][s * py_size:(s + 1) * py_size]
                        state = c * per + s
                        if x < 4:
                            send_back[pl.ds(state * 16 + x * 4 + y0 + i, py_size, stride=own * 16), :] = piece
                        else:
                            send_edge[pl.ds(state * 4 + y0 + i, py_size, stride=8), :] = piece

    def edge_copy(target):
        return send(block_of(send_edge, target, 8), block_of(edge, py, 8), 3, xn, target)

    def back_copy(target):
        return send(block_of(send_back, target, own * 16), block_of(result, py, own * 16), 4, px, target)

    over_all(edge_copy)
    over_others(back_copy)
    block_of(result, py, own * 16)[...] = block_of(send_back, py, own * 16)[...]
    edge_wait = pltpu.make_async_remote_copy(
        src_ref=edge, dst_ref=edge, send_sem=send_sem.at[3], recv_sem=recv_sem.at[3],
        device_id=(xn, py), device_id_type=MESH,
    )
    back_wait = pltpu.make_async_remote_copy(
        src_ref=spans.at[pl.ds(0, (py_size - 1) * own * 16)], dst_ref=result.at[pl.ds(0, (py_size - 1) * own * 16)],
        send_sem=send_sem.at[4], recv_sem=recv_sem.at[4], device_id=(xn, py), device_id_type=MESH,
    )
    edge_wait.wait_recv()
    back_wait.wait_recv()
    for s in range(own):
        for y in range(4):
            at = pl.ds(s * 16 + y, py_size, stride=own * 16)
            result[at, :] = result[at, :] + edge[pl.ds(s * 4 + y, py_size, stride=8), :]
    store = pltpu.make_async_copy(result, out_hbm, local_sem.at[0])
    store.start()
    for node in range(16):
        lhs[:, node * 128:(node + 1) * 128] = result[pl.ds(node, STATES, stride=16), :].astype(BF16)
    product = lax.dot_general(lhs[...], block_k[...], (((1,), (1,)), ((), ())), preferred_element_type=F32)
    for n in range(px_size):
        part[n] = product[n * tile_rows:(n + 1) * tile_rows]

    def first_copy(owner):
        return pltpu.make_async_remote_copy(
            src_ref=part.at[owner], dst_ref=got1.at[px], send_sem=send1, recv_sem=recv1,
            device_id=(owner, py), device_id_type=MESH,
        )

    for step in range(1, px_size):
        first_copy(lax.rem(px + step, px_size)).start()
    got1[px] = part[px]
    first_wait = pltpu.make_async_remote_copy(
        src_ref=part.at[0:px_size - 1], dst_ref=got1.at[0:px_size - 1], send_sem=send1, recv_sem=recv1,
        device_id=(xn, py), device_id_type=MESH,
    )
    first_wait.wait_recv()
    total = got1[0]
    for n in range(1, px_size):
        total = total + got1[n]
    sum1[0] = total[:, 0:128]
    sum1[1] = total[:, 128:256]

    def second_copy(target):
        return pltpu.make_async_remote_copy(
            src_ref=sum1.at[target // per_block], dst_ref=got2.at[py], send_sem=send2, recv_sem=recv2,
            device_id=(px, target), device_id_type=MESH,
        )

    over_others(second_copy)
    got2[py] = sum1[py // per_block]
    second_wait = pltpu.make_async_remote_copy(
        src_ref=got2.at[0:py_size - 1], dst_ref=got2.at[0:py_size - 1], send_sem=send2, recv_sem=recv2,
        device_id=(xn, py), device_id_type=MESH,
    )
    second_wait.wait_recv()
    total = got2[0]
    for n in range(1, py_size):
        total = total + got2[n]
    shift = lax.rem(128 - lax.rem(py, per_block) * tile_cols, 128)
    tile_ref[...] = pltpu.roll(total, shift, 1)[:, 0:tile_cols]

    store.wait()
    for wait in (block_wait, halo_wait, pot_wait, edge_wait, back_wait, first_wait, second_wait):
        wait.wait_send()
    for copies in sent:
        for copy in copies:
            copy.wait_send()


def local(px_size, py_size, span, potential, cell_matrix, block):
    chunks = CHUNKS
    own = STATES // py_size
    width = own // chunks * py_size
    rows = width
    field = pltpu.VMEM((chunks, 7, 5, rows, 128), F32)
    faces = pltpu.VMEM((chunks, 2, 4, rows, 128), F32)
    tile = (STATES // px_size, BLOCK // py_size)
    filtered, margin = pl.pallas_call(
        functools.partial(kernel, px_size, py_size, chunks),
        out_shape=(jax.ShapeDtypeStruct((STATES * 16, 128), F32), jax.ShapeDtypeStruct(tile, F32)),
        in_specs=[pl.BlockSpec(memory_space=pltpu.HBM)] * 4,
        out_specs=(pl.BlockSpec(memory_space=pltpu.HBM), pl.BlockSpec(memory_space=pltpu.VMEM)),
        scratch_shapes=[
            pltpu.VMEM((STATES * 16, 128), F32),
            pltpu.VMEM((125, 125), F32),
            pltpu.VMEM((128, 128), F32),
            pltpu.VMEM((BLOCK * 16, 128), BF16),
            pltpu.VMEM((BLOCK * 16, 128), F32),
            pltpu.VMEM((BLOCK, 2048), BF16),
            pltpu.VMEM((160, 480), BF16),
            pltpu.VMEM((4, 4, rows, 128), F32),
            pltpu.VMEM((STATES * 16, 128), F32),
            pltpu.VMEM((py_size, 16, 128), F32),
            pltpu.VMEM((py_size * 8, 128), F32),
            pltpu.VMEM((py_size * 8, 128), F32),
            field, field, field, field, field, field, faces, faces,
            pltpu.VMEM((STATES * 16, 128), F32),
            pltpu.VMEM((py_size * 8, 128), F32),
            pltpu.VMEM((py_size * 8, 128), F32),
            pltpu.VMEM((STATES * 16, 128), F32),
            pltpu.VMEM((STATES, 2048), BF16),
            pltpu.VMEM((px_size, tile[0], BLOCK), F32),
            pltpu.VMEM((px_size, tile[0], BLOCK), F32),
            pltpu.VMEM((2, tile[0], 128), F32),
            pltpu.VMEM((py_size, tile[0], 128), F32),
            pltpu.SemaphoreType.REGULAR,
            pltpu.SemaphoreType.DMA((4,)),
            pltpu.SemaphoreType.DMA((5,)),
            pltpu.SemaphoreType.DMA((5,)),
            pltpu.SemaphoreType.DMA((chunks, 4)),
            pltpu.SemaphoreType.DMA((chunks, 4)),
            pltpu.SemaphoreType.DMA,
            pltpu.SemaphoreType.DMA,
            pltpu.SemaphoreType.DMA,
            pltpu.SemaphoreType.DMA,
        ],
        compiler_params=pltpu.CompilerParams(
            collective_id=0, has_side_effects=True, vmem_limit_bytes=56 * 1024 * 1024
        ),
    )(span.reshape(STATES * 16, 128), potential.reshape(16, 128), cell_matrix, block.reshape(BLOCK * 16, 128))
    return filtered.reshape(span.shape), margin


def solution(mesh):
    in_specs = (P(None, "px", "py", None), P("px", "py", None), P(), P(None, "px", "py", None))
    out_specs = (P(None, "px", "py", None), P("px", "py"))
    body = functools.partial(local, mesh.shape["px"], mesh.shape["py"])
    return jax.shard_map(body, mesh=mesh, in_specs=in_specs, out_specs=out_specs, check_vma=False)
```

time: 69.4 us -> 67.4 us (0.971); the launches traced: 68.5 us -> 67.3 us
  local copies, waits for them, and re-layouts: 5.18 us -> 2.47 us
  Pallas kernels: 62.6 us -> 64.2 us
    unnamed x10 -> x4, local copies, waits for them, and re-layouts: 5.18 us -> 2.47 us
    pallas_call x1, Pallas kernels: 62.6 us -> 64.2 us  [local(): pl.pallas_call(functools.partial(kernel, px_size, py_size, chunks), out_s...]
where the time goes in v1:
time: 67.4 us; the launch traced here: 67.3 us
  Pallas kernels  64.2 us (95%)
  local copies, waits for them, and re-layouts  2.47 us (4%)
    pallas_call x1, Pallas kernels, local(): pl.pallas_call(functools.partial(kernel, px_size, py_size, chunks), out_s...  64.2 us
    unnamed x4, local copies, waits for them, and re-layouts  2.47 us

profile of v1, /device:TPU:1, one launch (start us, length us, event | category | flops | bytes accessed | tf_op | source)
XLA Modules:
  0.0 67.3 jit_solution(5570300722506600995)
XLA Ops:
  0.6 64.2 %shard_map.59 = (f32[1024,128]{1,0:T(8,128)}, f32[8,8]{1,0:T(8,128)}) custom-call(f32[1024,128]{1,0:T(8,128)} %bitcast.5, f32[16,128]{1,0:T(8,128)} %bitcast.7, f32[125,125]{1,0:T(8,128)} %mat_hbm.1, bf16[4096,128]{1,0:T(8,128)(2,1)} %bitcast.4), custom_call_target="tpu_custom_call" | custom-call | tf_op jit(solution)/shard_map/pallas_call | solution.py:438
  64.8 0.0 copy-start
  64.8 1.9 %copy.8 = f32[64,4,4,128]{3,2,1,0:T(4,128)} copy(f32[64,4,4,128]{3,2,1,0:T(4,128)} %bitcast.6) | data formatting | bytes 1048576
  66.7 0.0 copy-done
  66.7 0.6 copy.9
Async XLA Ops:
  64.8 1.9 %copy-start = (f32[8,8]{1,0:T(8,128)S(1)}, f32[8,8]{1,0:T(8,128)}, u32[]{:S(2)}) copy-start(f32[8,8]{1,0:T(8,128)} %get-tuple-element.9) | copy-start | bytes 772

commit v2 on v1

--- a/solution.py
+++ b/solution.py
@@ -12,7 +12,7 @@
 SCALE = 2.0 / 9.0
 F32 = jnp.float32
 BF16 = jnp.bfloat16
-CHUNKS = 1
+CHUNKS = 2
 STATES = 64
 BLOCK = 256
 
@@ -100,8 +100,10 @@
             device_id=(x, y), device_id_type=MESH,
         )
 
-    def span_copy(target):
-        return send(block_of(span_v, target, own * 16), block_of(spans, py, own * 16), 0, px, target)
+    def span_copy(c, target):
+        return send(
+            block_of(span_v, target * chunks + c, per * 16), block_of(spans.at[c], py, per * 16), 5 + c, px, target
+        )
 
     def halo_copy(target):
         return send(block_of(face_out, target, 8), block_of(halo, py, 8), 1, xp, target)
@@ -123,11 +125,13 @@
 
         lax.fori_loop(0, py_size, body, 0)
 
-    over_others(span_copy)
+    over_others(functools.partial(span_copy, 0))
     pl.semaphore_wait(ready, 2)
     over_all(halo_copy)
-    over_others(pot_copy)
-    block_of(spans, py, own * 16)[...] = block_of(span_v, py, own * 16)[...]
+    for c in range(1, chunks):
+        over_others(functools.partial(span_copy, c))
+    for c in range(chunks):
+        block_of(spans.at[c], py, per * 16)[...] = block_of(span_v, py * chunks + c, per * 16)[...]
 
     load_mat.wait()
     mat_pad[0:125, 0:125] = mat_v[...]
@@ -165,6 +169,8 @@
     for node in range(16):
         block_k[:, node * 128:(node + 1) * 128] = block_f[pl.ds(node, BLOCK, stride=16), :].astype(BF16)
 
+    over_others(pot_copy)
+
     lane = lax.broadcasted_iota(jnp.int32, (rows, 128), 1)
     first_cell = lax.rem(lane, py_size) == 0
     last_cell = lax.rem(lane, py_size) == py_size - 1
@@ -183,10 +189,8 @@
         turned = jnp.concatenate(rows_to_lanes(values, width), 0).T
         return [turned[i * width:(i + 1) * width] for i in range(groups)]
 
-    def states_of(ref, c, pitch, per_state, node):
-        loads = [
-            ref[pl.ds((c * per + s) * per_state + node, py_size, stride=pitch), :] for s in range(per)
-        ]
+    def states_of(ref, first, pitch):
+        loads = [ref[pl.ds(start, py_size, stride=pitch), :] for start in first]
         return jnp.concatenate(loads, 0) if per > 1 else loads[0]
 
     def flat(ref, c):
@@ -262,10 +266,13 @@
 
     faces = []
 
-    block_wait = pltpu.make_async_remote_copy(
-        src_ref=spans.at[pl.ds(0, (py_size - 1) * own * 16)], dst_ref=spans.at[pl.ds(0, (py_size - 1) * own * 16)],
-        send_sem=send_sem.at[0], recv_sem=recv_sem.at[0], device_id=(xn, py), device_id_type=MESH,
-    )
+    others = pl.ds(0, (py_size - 1) * per * 16)
+    block_waits = [
+        pltpu.make_async_remote_copy(
+            src_ref=spans.at[c, others], dst_ref=spans.at[c, others],
+            send_sem=send_sem.at[5 + c], recv_sem=recv_sem.at[5 + c], device_id=(xn, py), device_id_type=MESH,
+        ) for c in range(chunks)
+    ]
     halo_wait = pltpu.make_async_remote_copy(
         src_ref=halo, dst_ref=halo, send_sem=send_sem.at[1], recv_sem=recv_sem.at[1],
         device_id=(xn, py), device_id_type=MESH,
@@ -274,17 +281,22 @@
         src_ref=pots.at[0:py_size - 1], dst_ref=pots.at[0:py_size - 1], send_sem=send_sem.at[2],
         recv_sem=recv_sem.at[2], device_id=(xn, py), device_id_type=MESH,
     )
-    block_wait.wait_recv()
-    for c in range(chunks):
+    for c in range(chunks):
+        block_waits[c].wait_recv()
         for x in range(4):
             for y0 in range(0, 4, groups):
-                pieces = turn_in([states_of(spans, c, own * 16, 16, x * 4 + y0 + i) for i in range(groups)])
+                pieces = turn_in([
+                    states_of(spans.at[c], [s * 16 + x * 4 + y0 + i for s in range(per)], per * 16)
+                    for i in range(groups)
+                ])
                 for i in range(groups):
                     place(v0, c, x, y0 + i, pieces[i])
-    halo_wait.wait_recv()
-    for c in range(chunks):
+        if c == 0:
+            halo_wait.wait_recv()
         for y0 in range(0, 4, groups):
-            pieces = turn_in([states_of(halo, c, 8, 4, y0 + i) for i in range(groups)])
+            pieces = turn_in([
+                states_of(halo, [(c * per + s) * 4 + y0 + i for s in range(per)], 8) for i in range(groups)
+            ])
             for i in range(groups):
                 place(v0, c, 4, y0 + i, pieces[i])
         apply(v0, c1, c)
@@ -322,6 +334,15 @@
             for y in range(4):
                 place(v2, c, x, y, folded(c2, v1, c, x, y) - v0[c, x, y])
     sent = waiting + faces
+
+    def edge_copy(target):
+        return send(block_of(send_edge, target, 8), block_of(edge, py, 8), 3, xn, target)
+
+    def back_copy(c, target):
+        return send(
+            block_of(send_back.at[c], target, per * 16), block_of(result, py * chunks + c, per * 16),
+            5 + chunks + c, px, target,
+        )
 
     waiting = faces
     for c in range(chunks):
@@ -345,29 +366,29 @@
                         piece = pieces[i][s * py_size:(s + 1) * py_size]
                         state = c * per + s
                         if x < 4:
-                            send_back[pl.ds(state * 16 + x * 4 + y0 + i, py_size, stride=own * 16), :] = piece
+                            send_back[c, pl.ds(s * 16 + x * 4 + y0 + i, py_size, stride=per * 16), :] = piece
                         else:
                             send_edge[pl.ds(state * 4 + y0 + i, py_size, stride=8), :] = piece
 
-    def edge_copy(target):
-        return send(block_of(send_edge, target, 8), block_of(edge, py, 8), 3, xn, target)
-
-    def back_copy(target):
-        return send(block_of(send_back, target, own * 16), block_of(result, py, own * 16), 4, px, target)
-
-    over_all(edge_copy)
-    over_others(back_copy)
-    block_of(result, py, own * 16)[...] = block_of(send_back, py, own * 16)[...]
+        if c == chunks - 1:
+            over_all(edge_copy)
+        over_others(functools.partial(back_copy, c))
+        block_of(result, py * chunks + c, per * 16)[...] = block_of(send_back.at[c], py, per * 16)[...]
+
     edge_wait = pltpu.make_async_remote_copy(
         src_ref=edge, dst_ref=edge, send_sem=send_sem.at[3], recv_sem=recv_sem.at[3],
         device_id=(xn, py), device_id_type=MESH,
     )
-    back_wait = pltpu.make_async_remote_copy(
-        src_ref=spans.at[pl.ds(0, (py_size - 1) * own * 16)], dst_ref=result.at[pl.ds(0, (py_size - 1) * own * 16)],
-        send_sem=send_sem.at[4], recv_sem=recv_sem.at[4], device_id=(xn, py), device_id_type=MESH,
-    )
+    back_waits = [
+        pltpu.make_async_remote_copy(
+            src_ref=send_back.at[c, others], dst_ref=result.at[others],
+            send_sem=send_sem.at[5 + chunks + c], recv_sem=recv_sem.at[5 + chunks + c],
+            device_id=(xn, py), device_id_type=MESH,
+        ) for c in range(chunks)
+    ]
     edge_wait.wait_recv()
-    back_wait.wait_recv()
+    for wait in back_waits:
+        wait.wait_recv()
     for s in range(own):
         for y in range(4):
             at = pl.ds(s * 16 + y, py_size, stride=own * 16)
@@ -420,7 +441,7 @@
     tile_ref[...] = pltpu.roll(total, shift, 1)[:, 0:tile_cols]
 
     store.wait()
-    for wait in (block_wait, halo_wait, pot_wait, edge_wait, back_wait, first_wait, second_wait):
+    for wait in block_waits + [halo_wait, pot_wait, edge_wait] + back_waits + [first_wait, second_wait]:
         wait.wait_send()
     for copies in sent:
         for copy in copies:
@@ -439,7 +460,7 @@
         functools.partial(kernel, px_size, py_size, chunks),
         out_shape=(jax.ShapeDtypeStruct((STATES * 16, 128), F32), jax.ShapeDtypeStruct(tile, F32)),
         in_specs=[pl.BlockSpec(memory_space=pltpu.HBM)] * 4,
-        out_specs=(pl.BlockSpec(memory_space=pltpu.HBM), pl.BlockSpec(memory_space=pltpu.VMEM)),
+        out_specs=(pl.BlockSpec(memory_space=pl.ANY), pl.BlockSpec(memory_space=pltpu.VMEM)),
         scratch_shapes=[
             pltpu.VMEM((STATES * 16, 128), F32),
             pltpu.VMEM((125, 125), F32),
@@ -449,12 +470,12 @@
             pltpu.VMEM((BLOCK, 2048), BF16),
             pltpu.VMEM((160, 480), BF16),
             pltpu.VMEM((4, 4, rows, 128), F32),
-            pltpu.VMEM((STATES * 16, 128), F32),
+            pltpu.VMEM((chunks, STATES * 16 // chunks, 128), F32),
             pltpu.VMEM((py_size, 16, 128), F32),
             pltpu.VMEM((py_size * 8, 128), F32),
             pltpu.VMEM((py_size * 8, 128), F32),
             field, field, field, field, field, field, faces, faces,
-            pltpu.VMEM((STATES * 16, 128), F32),
+            pltpu.VMEM((chunks, STATES * 16 // chunks, 128), F32),
             pltpu.VMEM((py_size * 8, 128), F32),
             pltpu.VMEM((py_size * 8, 128), F32),
             pltpu.VMEM((STATES * 16, 128), F32),
@@ -465,8 +486,8 @@
             pltpu.VMEM((py_size, tile[0], 128), F32),
             pltpu.SemaphoreType.REGULAR,
             pltpu.SemaphoreType.DMA((4,)),
-            pltpu.SemaphoreType.DMA((5,)),
-            pltpu.SemaphoreType.DMA((5,)),
+            pltpu.SemaphoreType.DMA((5 + 2 * chunks,)),
+            pltpu.SemaphoreType.DMA((5 + 2 * chunks,)),
             pltpu.SemaphoreType.DMA((chunks, 4)),
             pltpu.SemaphoreType.DMA((chunks, 4)),
             pltpu.SemaphoreType.DMA,
@@ -475,9 +496,11 @@
             pltpu.SemaphoreType.DMA,
         ],
         compiler_params=pltpu.CompilerParams(
-            collective_id=0, has_side_effects=True, vmem_limit_bytes=56 * 1024 * 1024
+            collective_id=0, has_side_effects=True, vmem_limit_bytes=40 * 1024 * 1024
         ),
-    )(span.reshape(STATES * 16, 128), potential.reshape(16, 128), cell_matrix, block.reshape(BLOCK * 16, 128))
+    )(*(pltpu.with_memory_space_constraint(value, pltpu.HBM) for value in (
+        span.reshape(STATES * 16, 128), potential.reshape(16, 128), cell_matrix, block.reshape(BLOCK * 16, 128)
+    )))
     return filtered.reshape(span.shape), margin
 
 

time: 67.4 us -> 61.6 us (0.914)
  Pallas kernels: 64.2 us -> 59.4 us
  local copies, waits for them, and re-layouts: 2.47 us -> 1.39 us
    pallas_call x1, Pallas kernels: 64.2 us -> 59.4 us  [local(): pl.pallas_call(functools.partial(kernel, px_size, py_size, chunks), out_s...]
    unnamed x4 -> x2, local copies, waits for them, and re-layouts: 2.47 us -> 1.39 us
where the time goes in v2:
time: 61.6 us; the launch traced here: 61.5 us
  Pallas kernels  59.4 us (96%)
  local copies, waits for them, and re-layouts  1.39 us (2%)
  between operations  0.64 us (1%)
    pallas_call x1, Pallas kernels, local(): pl.pallas_call(functools.partial(kernel, px_size, py_size, chunks), out_s...  59.4 us
    unnamed x2, local copies, waits for them, and re-layouts  1.39 us

profile of v2, /device:TPU:1, one launch (start us, length us, event | category | flops | bytes accessed | tf_op | source)
XLA Modules:
  0.0 61.5 jit_solution(16175523455991699636)
XLA Ops:
  0.6 59.4 %shard_map.59 = (f32[1024,128]{1,0:T(8,128)S(1)}, f32[8,8]{1,0:T(8,128)S(1)}) custom-call(f32[1024,128]{1,0:T(8,128)} %bitcast.6, f32[16,128]{1,0:T(8,128)} %bitcast.7, f32[125,125]{1,0:T(8,128)} %mat_hbm.1, bf16[4096,128]{1,0:T(8,128)(2,1)} %bitcast.5), custom_call_target="tpu_custom_call" | custom-call | tf_op jit(solution)/shard_map/pallas_call | solution.py:459
  60.1 0.8 %copy.8 = f32[64,4,4,128]{3,2,1,0:T(4,128)} copy(f32[64,4,4,128]{3,2,1,0:T(4,128)S(1)} %bitcast.4) | data formatting | bytes 1048576
  60.9 0.6 copy.9

commit v3 on v2

--- a/solution.py
+++ b/solution.py
@@ -63,20 +63,19 @@
 
     barrier = pltpu.get_barrier_semaphore()
 
-    def greet_y(step, carry):
-        pl.semaphore_signal(
-            barrier, inc=1, device_id=(px, lax.rem(py + step, py_size)), device_id_type=MESH
-        )
-        return carry
-
-    def greet_x(step, carry):
-        pl.semaphore_signal(
-            barrier, inc=1, device_id=(lax.rem(px + step, px_size), py), device_id_type=MESH
-        )
-        return carry
-
-    lax.fori_loop(1, px_size, greet_x, 0)
-    lax.fori_loop(1, py_size, greet_y, 0)
+    z_part = [lax.rem(py // 16 + n, 2) * 16 for n in range(2)]
+    x_part = [lax.rem(lax.rem(py // 4, 4) + n, 4) * 4 for n in range(4)]
+    y_part = [lax.rem(lax.rem(py, 4) + n, 4) for n in range(4)]
+    offsets = [(z, x, y) for z in range(2) for x in range(4) for y in range(4)]
+    offsets.sort(key=lambda o: -(o[0] + min(o[1], 4 - o[1]) + min(o[2], 4 - o[2])))
+    group = [z_part[z] + x_part[x] + y_part[y] for z, x, y in offsets]
+    steps = sorted(range(1, px_size), key=lambda n: -min(n, px_size - n))
+    others_x = [lax.rem(px + n, px_size) for n in steps]
+
+    for x in others_x:
+        pl.semaphore_signal(barrier, inc=1, device_id=(x, py), device_id_type=MESH)
+    for y in group[:-1]:
+        pl.semaphore_signal(barrier, inc=1, device_id=(px, y), device_id_type=MESH)
     mat_pad[...] = jnp.zeros((128, 128), F32)
     load_mat.start()
     load_pot.start()
@@ -108,24 +107,20 @@
     def halo_copy(target):
         return send(block_of(face_out, target, 8), block_of(halo, py, 8), 1, xp, target)
 
-    def pot_copy(target):
-        return send(pot_hbm, pots.at[py], 2, px, target)
+    def pot_copy(first, target):
+        at = pl.ds(0, 4) if first else pl.ds(4, 12)
+        return send(pot_hbm.at[at], pots.at[py, at], 0 if first else 2, px, target)
 
     def over_others(make):
-        def body(step, carry):
-            make(lax.rem(py + step, py_size)).start()
-            return carry
-
-        lax.fori_loop(1, py_size, body, 0)
+        for target in group[:-1]:
+            make(target).start()
 
     def over_all(make):
-        def body(step, carry):
-            make(lax.rem(py + step, py_size)).start()
-            return carry
-
-        lax.fori_loop(0, py_size, body, 0)
+        for target in group:
+            make(target).start()
 
     over_others(functools.partial(span_copy, 0))
+    over_others(functools.partial(pot_copy, True))
     pl.semaphore_wait(ready, 2)
     over_all(halo_copy)
     for c in range(1, chunks):
@@ -169,7 +164,7 @@
     for node in range(16):
         block_k[:, node * 128:(node + 1) * 128] = block_f[pl.ds(node, BLOCK, stride=16), :].astype(BF16)
 
-    over_others(pot_copy)
+    over_others(functools.partial(pot_copy, False))
 
     lane = lax.broadcasted_iota(jnp.int32, (rows, 128), 1)
     first_cell = lax.rem(lane, py_size) == 0
@@ -277,10 +272,25 @@
         src_ref=halo, dst_ref=halo, send_sem=send_sem.at[1], recv_sem=recv_sem.at[1],
         device_id=(xn, py), device_id_type=MESH,
     )
-    pot_wait = pltpu.make_async_remote_copy(
-        src_ref=pots.at[0:py_size - 1], dst_ref=pots.at[0:py_size - 1], send_sem=send_sem.at[2],
-        recv_sem=recv_sem.at[2], device_id=(xn, py), device_id_type=MESH,
-    )
+    pot_waits = []
+    for slot, at in ((0, pl.ds(0, 4)), (2, pl.ds(4, 12))):
+        whole = pots.at[0:py_size - 1, at]
+        pot_waits.append(pltpu.make_async_remote_copy(
+            src_ref=whole, dst_ref=whole, send_sem=send_sem.at[slot], recv_sem=recv_sem.at[slot],
+            device_id=(xn, py), device_id_type=MESH,
+        ))
+
+    def turn_potential(x):
+        flat_pots = pots.reshape(py_size * 16, 128)
+        for y0 in range(0, 4, groups):
+            loads = []
+            for i in range(groups):
+                value = (flat_pots[pl.ds(x * 4 + y0 + i, py_size, stride=16), :] - CENTRE) * SCALE
+                loads += [value] * per
+            pieces = turn_in(loads)
+            for i in range(groups):
+                diag[x, y0 + i] = pieces[i]
+
     for c in range(chunks):
         block_waits[c].wait_recv()
         for x in range(4):
@@ -302,18 +312,12 @@
         apply(v0, c1, c)
         if c == 0:
             load_pot.wait()
-            pot_wait.wait_recv()
-            flat_pots = pots.reshape(py_size * 16, 128)
-            for x in range(4):
-                for y0 in range(0, 4, groups):
-                    loads = []
-                    for i in range(groups):
-                        value = (flat_pots[pl.ds(x * 4 + y0 + i, py_size, stride=16), :] - CENTRE) * SCALE
-                        loads += [value] * per
-                    pieces = turn_in(loads)
-                    for i in range(groups):
-                        diag[x, y0 + i] = pieces[i]
+            pot_waits[0].wait_recv()
+            turn_potential(0)
         faces.append(send_faces(c1, v0, r1, c, 0))
+    pot_waits[1].wait_recv()
+    for x in (1, 2, 3):
+        turn_potential(x)
     for c in range(chunks):
         for x in (1, 2, 3):
             for y in range(4):
@@ -335,8 +339,11 @@
                 place(v2, c, x, y, folded(c2, v1, c, x, y) - v0[c, x, y])
     sent = waiting + faces
 
-    def edge_copy(target):
-        return send(block_of(send_edge, target, 8), block_of(edge, py, 8), 3, xn, target)
+    def edge_copy(c, target):
+        return send(
+            block_of(send_edge.at[c], target, per * 4), block_of(edge, py * chunks + c, per * 4),
+            5 + 2 * chunks + c, xn, target,
+        )
 
     def back_copy(c, target):
         return send(
@@ -364,21 +371,22 @@
                 for i in range(groups):
                     for s in range(per):
                         piece = pieces[i][s * py_size:(s + 1) * py_size]
-                        state = c * per + s
                         if x < 4:
                             send_back[c, pl.ds(s * 16 + x * 4 + y0 + i, py_size, stride=per * 16), :] = piece
                         else:
-                            send_edge[pl.ds(state * 4 + y0 + i, py_size, stride=8), :] = piece
-
-        if c == chunks - 1:
-            over_all(edge_copy)
+                            send_edge[c, pl.ds(s * 4 + y0 + i, py_size, stride=per * 4), :] = piece
+
+        over_all(functools.partial(edge_copy, c))
         over_others(functools.partial(back_copy, c))
         block_of(result, py * chunks + c, per * 16)[...] = block_of(send_back.at[c], py, per * 16)[...]
 
-    edge_wait = pltpu.make_async_remote_copy(
-        src_ref=edge, dst_ref=edge, send_sem=send_sem.at[3], recv_sem=recv_sem.at[3],
-        device_id=(xn, py), device_id_type=MESH,
-    )
+    edge_waits = [
+        pltpu.make_async_remote_copy(
+            src_ref=send_edge.at[c], dst_ref=edge.at[0:py_size * per * 4],
+            send_sem=send_sem.at[5 + 2 * chunks + c], recv_sem=recv_sem.at[5 + 2 * chunks + c],
+            device_id=(xn, py), device_id_type=MESH,
+        ) for c in range(chunks)
+    ]
     back_waits = [
         pltpu.make_async_remote_copy(
             src_ref=send_back.at[c, others], dst_ref=result.at[others],
@@ -386,7 +394,8 @@
             device_id=(xn, py), device_id_type=MESH,
         ) for c in range(chunks)
     ]
-    edge_wait.wait_recv()
+    for wait in edge_waits:
+        wait.wait_recv()
     for wait in back_waits:
         wait.wait_recv()
     for s in range(own):
@@ -407,8 +416,8 @@
             device_id=(owner, py), device_id_type=MESH,
         )
 
-    for step in range(1, px_size):
-        first_copy(lax.rem(px + step, px_size)).start()
+    for owner in others_x:
+        first_copy(owner).start()
     got1[px] = part[px]
     first_wait = pltpu.make_async_remote_copy(
         src_ref=part.at[0:px_size - 1], dst_ref=got1.at[0:px_size - 1], send_sem=send1, recv_sem=recv1,
@@ -441,7 +450,7 @@
     tile_ref[...] = pltpu.roll(total, shift, 1)[:, 0:tile_cols]
 
     store.wait()
-    for wait in block_waits + [halo_wait, pot_wait, edge_wait] + back_waits + [first_wait, second_wait]:
+    for wait in block_waits + [halo_wait] + pot_waits + edge_waits + back_waits + [first_wait, second_wait]:
         wait.wait_send()
     for copies in sent:
         for copy in copies:
@@ -476,7 +485,7 @@
             pltpu.VMEM((py_size * 8, 128), F32),
             field, field, field, field, field, field, faces, faces,
             pltpu.VMEM((chunks, STATES * 16 // chunks, 128), F32),
-            pltpu.VMEM((py_size * 8, 128), F32),
+            pltpu.VMEM((chunks, py_size * 8 // chunks, 128), F32),
             pltpu.VMEM((py_size * 8, 128), F32),
             pltpu.VMEM((STATES * 16, 128), F32),
             pltpu.VMEM((STATES, 2048), BF16),
@@ -486,8 +495,8 @@
             pltpu.VMEM((py_size, tile[0], 128), F32),
             pltpu.SemaphoreType.REGULAR,
             pltpu.SemaphoreType.DMA((4,)),
-            pltpu.SemaphoreType.DMA((5 + 2 * chunks,)),
-            pltpu.SemaphoreType.DMA((5 + 2 * chunks,)),
+            pltpu.SemaphoreType.DMA((5 + 3 * chunks,)),
+            pltpu.SemaphoreType.DMA((5 + 3 * chunks,)),
             pltpu.SemaphoreType.DMA((chunks, 4)),
             pltpu.SemaphoreType.DMA((chunks, 4)),
             pltpu.SemaphoreType.DMA,

time: 61.6 us -> 58.4 us (0.948)
  Pallas kernels: 59.4 us -> 56.3 us
    pallas_call x1, Pallas kernels: 59.4 us -> 56.3 us  [local(): pl.pallas_call(functools.partial(kernel, px_size, py_size, chunks), out_s...]
where the time goes in v3:
time: 58.4 us; the launch traced here: 58.3 us
  Pallas kernels  56.3 us (96%)
  local copies, waits for them, and re-layouts  1.39 us (2%)
  between operations  0.64 us (1%)
    pallas_call x1, Pallas kernels, local(): pl.pallas_call(functools.partial(kernel, px_size, py_size, chunks), out_s...  56.3 us
    unnamed x2, local copies, waits for them, and re-layouts  1.39 us

profile of v3, /device:TPU:1, one launch (start us, length us, event | category | flops | bytes accessed | tf_op | source)
XLA Modules:
  0.0 58.3 jit_solution(18276660867886516250)
XLA Ops:
  0.6 56.3 %shard_map.59 = (f32[1024,128]{1,0:T(8,128)S(1)}, f32[8,8]{1,0:T(8,128)S(1)}) custom-call(f32[1024,128]{1,0:T(8,128)} %bitcast.6, f32[16,128]{1,0:T(8,128)} %bitcast.7, f32[125,125]{1,0:T(8,128)} %mat_hbm.1, bf16[4096,128]{1,0:T(8,128)(2,1)} %bitcast.5), custom_call_target="tpu_custom_call" | custom-call | tf_op jit(solution)/shard_map/pallas_call | solution.py:468
  56.9 0.8 %copy.8 = f32[64,4,4,128]{3,2,1,0:T(4,128)} copy(f32[64,4,4,128]{3,2,1,0:T(4,128)S(1)} %bitcast.4) | data formatting | bytes 1048576
  57.7 0.6 %copy.9 = f32[8,8]{1,0:T(8,128)} copy(f32[8,8]{1,0:T(8,128)S(1)} %get-tuple-element.9) | data formatting | bytes 512

commit v4 on v3

--- a/solution.py
+++ b/solution.py
@@ -38,7 +38,7 @@
     px_size, py_size, chunks,
     span_hbm, pot_hbm, mat_hbm, block_hbm,
     out_hbm, tile_ref,
-    span_v, mat_v, mat_pad, block_v, block_f, block_k, mat3, diag,
+    span_v, packed, mat_v, mat_pad, block_v, block_f, block_k, mat3, diag,
     spans, pots, halo, face_out,
     v0, v1, v2, c1, c2, c3, r1, r2,
     send_back, send_edge, edge, result, lhs, part, got1, sum1, got2,
@@ -49,11 +49,11 @@
     width = per * py_size
     groups = 128 // width
     rows = 128 // groups
+    pitch = [per * 16 + 4] + [per * 16] * (chunks - 1)
     px, py = lax.axis_index("px"), lax.axis_index("py")
     xn, xp = lax.rem(px + 1, px_size), lax.rem(px + px_size - 1, px_size)
     tile_rows = STATES // px_size
     tile_cols = BLOCK // py_size
-    per_block = 128 // tile_cols
 
     load_span = pltpu.make_async_copy(span_hbm, span_v, local_sem.at[0])
     load_block = pltpu.make_async_copy(block_hbm, block_v, local_sem.at[1])
@@ -67,16 +67,22 @@
     x_part = [lax.rem(lax.rem(py // 4, 4) + n, 4) * 4 for n in range(4)]
     y_part = [lax.rem(lax.rem(py, 4) + n, 4) for n in range(4)]
     offsets = [(z, x, y) for z in range(2) for x in range(4) for y in range(4)]
-    offsets.sort(key=lambda o: -(o[0] + min(o[1], 4 - o[1]) + min(o[2], 4 - o[2])))
+    offsets.sort(key=lambda o: (o == (0, 0, 0), -o[0], -(o[0] + min(o[1], 4 - o[1]) + min(o[2], 4 - o[2]))))
     group = [z_part[z] + x_part[x] + y_part[y] for z, x, y in offsets]
     steps = sorted(range(1, px_size), key=lambda n: -min(n, px_size - n))
     others_x = [lax.rem(px + n, px_size) for n in steps]
+    plane = lax.rem(py, 16)
+    z_own = py // 16
+    plane_group = [x_part[x] + y_part[y] for z, x, y in offsets if z == 0][:-1]
+    column_group = [(x, lax.rem(z_own + n, 2)) for x in others_x for n in (1, 0)] + [(px, lax.rem(z_own + 1, 2))]
 
     for x in others_x:
-        pl.semaphore_signal(barrier, inc=1, device_id=(x, py), device_id_type=MESH)
+        for y in (py, z_part[1] + plane):
+            pl.semaphore_signal(barrier, inc=1, device_id=(x, y), device_id_type=MESH)
     for y in group[:-1]:
         pl.semaphore_signal(barrier, inc=1, device_id=(px, y), device_id_type=MESH)
     mat_pad[...] = jnp.zeros((128, 128), F32)
+    part[...] = jnp.zeros(part.shape, F32)
     load_mat.start()
     load_pot.start()
     load_block.start()
@@ -86,7 +92,15 @@
         for y in range(4):
             face_out[pl.ds(s * 4 + y, py_size, stride=8), :] = span_v[pl.ds(s * 16 + y, py_size, stride=own * 16), :]
 
-    pl.semaphore_wait(barrier, (px_size - 1) + (py_size - 1))
+    for r in range(per * 16):
+        packed[pl.ds(r, py_size, stride=pitch[0]), :] = span_v[pl.ds(r, py_size, stride=own * 16), :]
+    load_pot.wait()
+    for y in range(4):
+        packed[pl.ds(per * 16 + y, py_size, stride=pitch[0]), :] = jnp.broadcast_to(
+            pots[py, y:y + 1, :], (py_size, 128)
+        )
+
+    pl.semaphore_wait(barrier, 2 * (px_size - 1) + (py_size - 1))
     for x in (xn, xp):
         pl.semaphore_signal(ready, inc=1, device_id=(x, py), device_id_type=MESH)
 
@@ -100,6 +114,8 @@
         )
 
     def span_copy(c, target):
+        if c == 0:
+            return send(block_of(packed, target, pitch[0]), block_of(spans.at[0], py, pitch[0]), 5, px, target)
         return send(
             block_of(span_v, target * chunks + c, per * 16), block_of(spans.at[c], py, per * 16), 5 + c, px, target
         )
@@ -107,9 +123,9 @@
     def halo_copy(target):
         return send(block_of(face_out, target, 8), block_of(halo, py, 8), 1, xp, target)
 
-    def pot_copy(first, target):
-        at = pl.ds(0, 4) if first else pl.ds(4, 12)
-        return send(pot_hbm.at[at], pots.at[py, at], 0 if first else 2, px, target)
+    def pot_copy(target):
+        at = pl.ds(4, 12)
+        return send(pot_hbm.at[at], pots.at[py, at], 2, px, target)
 
     def over_others(make):
         for target in group[:-1]:
@@ -120,12 +136,12 @@
             make(target).start()
 
     over_others(functools.partial(span_copy, 0))
-    over_others(functools.partial(pot_copy, True))
     pl.semaphore_wait(ready, 2)
     over_all(halo_copy)
     for c in range(1, chunks):
         over_others(functools.partial(span_copy, c))
-    for c in range(chunks):
+    spans[0, pl.ds(py * pitch[0], pitch[0]), :] = packed[pl.ds(py * pitch[0], pitch[0]), :]
+    for c in range(1, chunks):
         block_of(spans.at[c], py, per * 16)[...] = block_of(span_v, py * chunks + c, per * 16)[...]
 
     load_mat.wait()
@@ -164,7 +180,7 @@
     for node in range(16):
         block_k[:, node * 128:(node + 1) * 128] = block_f[pl.ds(node, BLOCK, stride=16), :].astype(BF16)
 
-    over_others(functools.partial(pot_copy, False))
+    over_others(pot_copy)
 
     lane = lax.broadcasted_iota(jnp.int32, (rows, 128), 1)
     first_cell = lax.rem(lane, py_size) == 0
@@ -264,7 +280,7 @@
     others = pl.ds(0, (py_size - 1) * per * 16)
     block_waits = [
         pltpu.make_async_remote_copy(
-            src_ref=spans.at[c, others], dst_ref=spans.at[c, others],
+            src_ref=spans.at[c, 0:(py_size - 1) * pitch[c]], dst_ref=spans.at[c, 0:(py_size - 1) * pitch[c]],
             send_sem=send_sem.at[5 + c], recv_sem=recv_sem.at[5 + c], device_id=(xn, py), device_id_type=MESH,
         ) for c in range(chunks)
     ]
@@ -272,20 +288,22 @@
         src_ref=halo, dst_ref=halo, send_sem=send_sem.at[1], recv_sem=recv_sem.at[1],
         device_id=(xn, py), device_id_type=MESH,
     )
-    pot_waits = []
-    for slot, at in ((0, pl.ds(0, 4)), (2, pl.ds(4, 12))):
-        whole = pots.at[0:py_size - 1, at]
-        pot_waits.append(pltpu.make_async_remote_copy(
-            src_ref=whole, dst_ref=whole, send_sem=send_sem.at[slot], recv_sem=recv_sem.at[slot],
-            device_id=(xn, py), device_id_type=MESH,
-        ))
+    rest = pots.at[0:py_size - 1, 4:16]
+    pot_wait = pltpu.make_async_remote_copy(
+        src_ref=rest, dst_ref=rest, send_sem=send_sem.at[2], recv_sem=recv_sem.at[2],
+        device_id=(xn, py), device_id_type=MESH,
+    )
 
     def turn_potential(x):
         flat_pots = pots.reshape(py_size * 16, 128)
         for y0 in range(0, 4, groups):
             loads = []
             for i in range(groups):
-                value = (flat_pots[pl.ds(x * 4 + y0 + i, py_size, stride=16), :] - CENTRE) * SCALE
+                if x == 0:
+                    value = spans[0, pl.ds(per * 16 + y0 + i, py_size, stride=pitch[0]), :]
+                else:
+                    value = flat_pots[pl.ds(x * 4 + y0 + i, py_size, stride=16), :]
+                value = (value - CENTRE) * SCALE
                 loads += [value] * per
             pieces = turn_in(loads)
             for i in range(groups):
@@ -296,7 +314,7 @@
         for x in range(4):
             for y0 in range(0, 4, groups):
                 pieces = turn_in([
-                    states_of(spans.at[c], [s * 16 + x * 4 + y0 + i for s in range(per)], per * 16)
+                    states_of(spans.at[c], [s * 16 + x * 4 + y0 + i for s in range(per)], pitch[c])
                     for i in range(groups)
                 ])
                 for i in range(groups):
@@ -311,11 +329,9 @@
                 place(v0, c, 4, y0 + i, pieces[i])
         apply(v0, c1, c)
         if c == 0:
-            load_pot.wait()
-            pot_waits[0].wait_recv()
             turn_potential(0)
         faces.append(send_faces(c1, v0, r1, c, 0))
-    pot_waits[1].wait_recv()
+    pot_wait.wait_recv()
     for x in (1, 2, 3):
         turn_potential(x)
     for c in range(chunks):
@@ -406,51 +422,52 @@
     store.start()
     for node in range(16):
         lhs[:, node * 128:(node + 1) * 128] = result[pl.ds(node, STATES, stride=16), :].astype(BF16)
-    product = lax.dot_general(lhs[...], block_k[...], (((1,), (1,)), ((), ())), preferred_element_type=F32)
-    for n in range(px_size):
-        part[n] = product[n * tile_rows:(n + 1) * tile_rows]
-
-    def first_copy(owner):
+    product = lax.dot_general(block_k[...], lhs[...], (((1,), (1,)), ((), ())), preferred_element_type=F32)
+    for n in range(py_size):
+        part[n // 16, n % 16, :, 0:STATES] = product[n * tile_cols:(n + 1) * tile_cols]
+
+    def first_copy(target):
         return pltpu.make_async_remote_copy(
-            src_ref=part.at[owner], dst_ref=got1.at[px], send_sem=send1, recv_sem=recv1,
-            device_id=(owner, py), device_id_type=MESH,
-        )
-
-    for owner in others_x:
-        first_copy(owner).start()
-    got1[px] = part[px]
+            src_ref=part.at[:, target], dst_ref=got1.at[plane], send_sem=send1, recv_sem=recv1,
+            device_id=(px, z_part[0] + target), device_id_type=MESH,
+        )
+
+    for target in plane_group:
+        first_copy(target).start()
+    got1[plane] = part[:, plane]
     first_wait = pltpu.make_async_remote_copy(
-        src_ref=part.at[0:px_size - 1], dst_ref=got1.at[0:px_size - 1], send_sem=send1, recv_sem=recv1,
+        src_ref=got1.at[0:15], dst_ref=got1.at[0:15], send_sem=send1, recv_sem=recv1,
         device_id=(xn, py), device_id_type=MESH,
     )
     first_wait.wait_recv()
     total = got1[0]
-    for n in range(1, px_size):
+    for n in range(1, 16):
         total = total + got1[n]
-    sum1[0] = total[:, 0:128]
-    sum1[1] = total[:, 128:256]
-
-    def second_copy(target):
+    sum1[...] = total
+
+    def second_copy(x, z):
         return pltpu.make_async_remote_copy(
-            src_ref=sum1.at[target // per_block], dst_ref=got2.at[py], send_sem=send2, recv_sem=recv2,
-            device_id=(px, target), device_id_type=MESH,
-        )
-
-    over_others(second_copy)
-    got2[py] = sum1[py // per_block]
+            src_ref=sum1.at[z], dst_ref=got2.at[px * 2 + z_own], send_sem=send2, recv_sem=recv2,
+            device_id=(x, z * 16 + plane), device_id_type=MESH,
+        )
+
+    for x, z in column_group:
+        second_copy(x, z).start()
+    got2[px * 2 + z_own] = sum1[z_own]
     second_wait = pltpu.make_async_remote_copy(
-        src_ref=got2.at[0:py_size - 1], dst_ref=got2.at[0:py_size - 1], send_sem=send2, recv_sem=recv2,
+        src_ref=got2.at[0:2 * px_size - 1], dst_ref=got2.at[0:2 * px_size - 1], send_sem=send2, recv_sem=recv2,
         device_id=(xn, py), device_id_type=MESH,
     )
     second_wait.wait_recv()
     total = got2[0]
-    for n in range(1, py_size):
+    for n in range(1, 2 * px_size):
         total = total + got2[n]
-    shift = lax.rem(128 - lax.rem(py, per_block) * tile_cols, 128)
-    tile_ref[...] = pltpu.roll(total, shift, 1)[:, 0:tile_cols]
+    total = pltpu.roll(total, lax.rem(128 - px * tile_rows, 128), 1)
+    total = jnp.concatenate([total, jnp.zeros((128 - tile_cols, 128), F32)], 0).T
+    tile_ref[...] = total[0:tile_rows, 0:tile_cols]
 
     store.wait()
-    for wait in block_waits + [halo_wait] + pot_waits + edge_waits + back_waits + [first_wait, second_wait]:
+    for wait in block_waits + [halo_wait, pot_wait] + edge_waits + back_waits + [first_wait, second_wait]:
         wait.wait_send()
     for copies in sent:
         for copy in copies:
@@ -472,6 +489,7 @@
         out_specs=(pl.BlockSpec(memory_space=pl.ANY), pl.BlockSpec(memory_space=pltpu.VMEM)),
         scratch_shapes=[
             pltpu.VMEM((STATES * 16, 128), F32),
+            pltpu.VMEM((py_size * (width // py_size * 16 + 4), 128), F32),
             pltpu.VMEM((125, 125), F32),
             pltpu.VMEM((128, 128), F32),
             pltpu.VMEM((BLOCK * 16, 128), BF16),
@@ -479,7 +497,7 @@
             pltpu.VMEM((BLOCK, 2048), BF16),
             pltpu.VMEM((160, 480), BF16),
             pltpu.VMEM((4, 4, rows, 128), F32),
-            pltpu.VMEM((chunks, STATES * 16 // chunks, 128), F32),
+            pltpu.VMEM((chunks, py_size * (width // py_size * 16 + 4), 128), F32),
             pltpu.VMEM((py_size, 16, 128), F32),
             pltpu.VMEM((py_size * 8, 128), F32),
             pltpu.VMEM((py_size * 8, 128), F32),
@@ -489,10 +507,10 @@
             pltpu.VMEM((py_size * 8, 128), F32),
             pltpu.VMEM((STATES * 16, 128), F32),
             pltpu.VMEM((STATES, 2048), BF16),
-            pltpu.VMEM((px_size, tile[0], BLOCK), F32),
-            pltpu.VMEM((px_size, tile[0], BLOCK), F32),
-            pltpu.VMEM((2, tile[0], 128), F32),
-            pltpu.VMEM((py_size, tile[0], 128), F32),
+            pltpu.VMEM((2, 16, tile[1], 128), F32),
+            pltpu.VMEM((16, 2, tile[1], 128), F32),
+            pltpu.VMEM((2, tile[1], 128), F32),
+            pltpu.VMEM((2 * px_size, tile[1], 128), F32),
             pltpu.SemaphoreType.REGULAR,
             pltpu.SemaphoreType.DMA((4,)),
             pltpu.SemaphoreType.DMA((5 + 3 * chunks,)),

time: 58.4 us -> 57.6 us (0.986)
  Pallas kernels: 56.3 us -> 55.5 us
    pallas_call x1, Pallas kernels: 56.3 us -> 55.5 us  [local(): pl.pallas_call(functools.partial(kernel, px_size, py_size, chunks), out_s...]
where the time goes in v4:
time: 57.6 us; the launch traced here: 57.5 us
  Pallas kernels  55.5 us (96%)
  local copies, waits for them, and re-layouts  1.39 us (2%)
  between operations  0.64 us (1%)
    pallas_call x1, Pallas kernels, local(): pl.pallas_call(functools.partial(kernel, px_size, py_size, chunks), out_s...  55.5 us
    unnamed x2, local copies, waits for them, and re-layouts  1.39 us

profile of v4, /device:TPU:1, one launch (start us, length us, event | category | flops | bytes accessed | tf_op | source)
XLA Modules:
  0.0 57.5 jit_solution(5956295478658161537)
XLA Ops:
  0.6 55.5 %shard_map.59 = (f32[1024,128]{1,0:T(8,128)S(1)}, f32[8,8]{1,0:T(8,128)S(1)}) custom-call(f32[1024,128]{1,0:T(8,128)} %bitcast.6, f32[16,128]{1,0:T(8,128)} %bitcast.7, f32[125,125]{1,0:T(8,128)} %mat_hbm.1, bf16[4096,128]{1,0:T(8,128)(2,1)} %bitcast.5), custom_call_target="tpu_custom_call" | custom-call | tf_op jit(solution)/shard_map/pallas_call | solution.py:485
  56.1 0.8 %copy.8 = f32[64,4,4,128]{3,2,1,0:T(4,128)} copy(f32[64,4,4,128]{3,2,1,0:T(4,128)S(1)} %bitcast.4) | data formatting | bytes 1048576
  56.9 0.6 %copy.9 = f32[8,8]{1,0:T(8,128)} copy(f32[8,8]{1,0:T(8,128)S(1)} %get-tuple-element.9) | data formatting | bytes 512

commit v5 on v4

--- a/solution.py
+++ b/solution.py
@@ -135,9 +135,12 @@
         for target in group:
             make(target).start()
 
-    over_others(functools.partial(span_copy, 0))
+    for target in group[:16]:
+        span_copy(0, target).start()
     pl.semaphore_wait(ready, 2)
     over_all(halo_copy)
+    for target in group[16:-1]:
+        span_copy(0, target).start()
     for c in range(1, chunks):
         over_others(functools.partial(span_copy, c))
     spans[0, pl.ds(py * pitch[0], pitch[0]), :] = packed[pl.ds(py * pitch[0], pitch[0]), :]
@@ -180,7 +183,6 @@
     for node in range(16):
         block_k[:, node * 128:(node + 1) * 128] = block_f[pl.ds(node, BLOCK, stride=16), :].astype(BF16)
 
-    over_others(pot_copy)
 
     lane = lax.broadcasted_iota(jnp.int32, (rows, 128), 1)
     first_cell = lax.rem(lane, py_size) == 0
@@ -311,6 +313,8 @@
 
     for c in range(chunks):
         block_waits[c].wait_recv()
+        if c == 0:
+            over_others(pot_copy)
         for x in range(4):
             for y0 in range(0, 4, groups):
                 pieces = turn_in([

time: 57.6 us -> 58.1 us (level)
  no operation moved by 1% of the time
where the time goes in v5:
time: 58.1 us; the launch traced here: 58 us
  Pallas kernels  55.9 us (96%)
  local copies, waits for them, and re-layouts  1.39 us (2%)
  between operations  0.64 us (1%)
    pallas_call x1, Pallas kernels, local(): pl.pallas_call(functools.partial(kernel, px_size, py_size, chunks), out_s...  55.9 us
    unnamed x2, local copies, waits for them, and re-layouts  1.39 us

profile of v5, /device:TPU:1, one launch (start us, length us, event | category | flops | bytes accessed | tf_op | source)
XLA Modules:
  0.0 58.0 jit_solution(12420165448906249615)
XLA Ops:
  0.6 55.9 %shard_map.59 = (f32[1024,128]{1,0:T(8,128)S(1)}, f32[8,8]{1,0:T(8,128)S(1)}) custom-call(f32[1024,128]{1,0:T(8,128)} %bitcast.6, f32[16,128]{1,0:T(8,128)} %bitcast.7, f32[125,125]{1,0:T(8,128)} %mat_hbm.1, bf16[4096,128]{1,0:T(8,128)(2,1)} %bitcast.5), custom_call_target="tpu_custom_call" | custom-call | tf_op jit(solution)/shard_map/pallas_call | solution.py:489
  56.6 0.8 %copy.8 = f32[64,4,4,128]{3,2,1,0:T(4,128)} copy(f32[64,4,4,128]{3,2,1,0:T(4,128)S(1)} %bitcast.4) | data formatting | bytes 1048576
  57.4 0.6 %copy.9 = f32[8,8]{1,0:T(8,128)} copy(f32[8,8]{1,0:T(8,128)S(1)} %get-tuple-element.9) | data formatting | bytes 512

commit v6 on v5

--- a/solution.py
+++ b/solution.py
@@ -183,6 +183,7 @@
     for node in range(16):
         block_k[:, node * 128:(node + 1) * 128] = block_f[pl.ds(node, BLOCK, stride=16), :].astype(BF16)
 
+    over_others(pot_copy)
 
     lane = lax.broadcasted_iota(jnp.int32, (rows, 128), 1)
     first_cell = lax.rem(lane, py_size) == 0
@@ -313,8 +314,6 @@
 
     for c in range(chunks):
         block_waits[c].wait_recv()
-        if c == 0:
-            over_others(pot_copy)
         for x in range(4):
             for y0 in range(0, 4, groups):
                 pieces = turn_in([

time: 58.1 us -> 57.7 us (level)
  no operation moved by 1% of the time
where the time goes in v6:
time: 57.7 us; the launch traced here: 57.6 us
  Pallas kernels  55.5 us (96%)
  local copies, waits for them, and re-layouts  1.39 us (2%)
  between operations  0.64 us (1%)
    pallas_call x1, Pallas kernels, local(): pl.pallas_call(functools.partial(kernel, px_size, py_size, chunks), out_s...  55.5 us
    unnamed x2, local copies, waits for them, and re-layouts  1.39 us

profile of v6, /device:TPU:1, one launch (start us, length us, event | category | flops | bytes accessed | tf_op | source)
XLA Modules:
  0.0 57.6 jit_solution(4474072657095619308)
XLA Ops:
  0.6 55.5 %shard_map.59 = (f32[1024,128]{1,0:T(8,128)S(1)}, f32[8,8]{1,0:T(8,128)S(1)}) custom-call(f32[1024,128]{1,0:T(8,128)} %bitcast.6, f32[16,128]{1,0:T(8,128)} %bitcast.7, f32[125,125]{1,0:T(8,128)} %mat_hbm.1, bf16[4096,128]{1,0:T(8,128)(2,1)} %bitcast.5), custom_call_target="tpu_custom_call" | custom-call | tf_op jit(solution)/shard_map/pallas_call | solution.py:488
  56.2 0.8 %copy.8 = f32[64,4,4,128]{3,2,1,0:T(4,128)} copy(f32[64,4,4,128]{3,2,1,0:T(4,128)S(1)} %bitcast.4) | data formatting | bytes 1048576
  57.0 0.6 %copy.9 = f32[8,8]{1,0:T(8,128)} copy(f32[8,8]{1,0:T(8,128)S(1)} %get-tuple-element.9) | data formatting | bytes 512
